TPU v7x, 32 devices: a whole 2x2x4 slice. The times are simulated.
32 devices in a mesh: grp: 2 (over x), ctx: 4 (over z), wsh: 4 (over y, core).
Axes of the slice: x: 2, y: 2, z: 4, core: 2. Of those that a mesh axis runs over, the one named last changes fastest.
Arguments:
- inputs: bfloat16 [2, 4, 2048, 1024], P('grp', 'wsh', 'ctx'), may hold values from -6 to 6
- w_qkv: bfloat16 [1024, 3072], P('wsh'), may hold values from -0.1875 to 0.1875
- w_out: bfloat16 [1024, 1024], P('wsh'), may hold values from -0.1875 to 0.1875
- w_up: bfloat16 [1024, 4096], P('wsh'), may hold values from -0.1875 to 0.1875
- w_down: bfloat16 [4096, 1024], P('wsh'), may hold values from -0.09375 to 0.09375
- norm_gains: float32 [4, 1024], replicated, may hold values from 0.5 to 1.5
- norm_biases: float32 [4, 1024], replicated, may hold values from -2 to 2
- block_map: int32 [2, 4, 4, 2], P('grp', 'wsh', 'ctx'), may hold values from 0 to 1024, as said below
- out_grad: bfloat16 [2, 4, 2048, 1024], P('grp', 'wsh', 'ctx'), may hold values from -6 to 6
Outputs:
- output: bfloat16 [2, 4, 2048, 1024], P('grp', 'wsh', 'ctx')
- input_grad: float32 [2, 4, 2048, 1024], P('grp', 'wsh', 'ctx')
- grad_qkv: float32 [1024, 3072], P('wsh')
- grad_attn_out: float32 [1024, 1024], P('wsh')
- grad_up: float32 [1024, 4096], P('wsh')
- grad_down: float32 [4096, 1024], P('wsh')
- grad_gains: float32 [4, 1024], replicated
- grad_biases: float32 [4, 1024], replicated
Inputs may be any that keep to these rules, and one draw needn't show every extreme that they name: `block_map`: for each grp and wsh index the 4 context blocks are the 2 prompt blocks (sequence 0, first positions 0, 512, 1024 and so on) and one block of each continuation 1 to 4 // 2 (first position 1024), in an order drawn for each family.
All inputs are finite; a program needn't handle non-finite values.
Results may differ from a plain program's by a relative error of at most 0.017.
Values may be sent and summed in bfloat16 or wider, within the bound.
A program may use at most 384 MiB of HBM per device.

v0:
```python
import math
import jax
import jax.numpy as jnp
from jax import lax
from jax.sharding import PartitionSpec as P

D = 1024
HEADS = 16
DH = 64
BLK = 512
EPS = 1e-05
ALPHA = 32.0
NEG = -1e30


def layer_norm(values, gain_row, bias_row):
    centre = values - jnp.mean(values, axis=-1, keepdims=True)
    spread = jnp.mean(centre * centre, axis=-1, keepdims=True)
    return centre * lax.rsqrt(spread + EPS) * gain_row + bias_row


def gelu_tanh(values):
    return jax.nn.gelu(values, approximate=True)


def contract_last(left_side, right_side):
    return lax.dot_general(
        left_side, right_side, (((1,), (1,)), ((), ())), preferred_element_type=jnp.float32
    )


def contract_rows(left_side, right_side):
    return lax.dot_general(
        left_side, right_side, (((0,), (0,)), ((), ())), preferred_element_type=jnp.float32
    )


def allowed(query_tags, key_tags):
    same_doc = (key_tags[None, :, 0] == query_tags[:, None, 0]) | (key_tags[None, :, 0] == 0)
    return same_doc & (key_tags[None, :, 1] <= query_tags[:, None, 1])


def scores(queries, key_block, permit):
    raw_scores = jnp.einsum("qhd,khd->hqk", queries, key_block, preferred_element_type=jnp.float32)
    return jnp.where(permit[None], raw_scores * ALPHA, NEG)


def no_output(step_rows):
    return None


def zero_terms(step_rows):
    zero_rows = jnp.zeros((step_rows, HEADS, DH), jnp.float32)
    return (zero_rows, zero_rows)


def sweep_blocks(members, query_tags, state, update, blank):
    total_rows = members[0].shape[0]
    limit_rows = max(query_tags.shape[0], 512)
    block_count = total_rows // limit_rows
    stacked = tuple(
        (member.reshape((block_count, limit_rows) + member.shape[1:]) for member in members)
    )

    def advance(held_state, pieces):
        permit = allowed(query_tags, pieces[-1])

        def active(inner_state):
            return update(inner_state, pieces, permit)

        def passive(inner_state):
            return (inner_state, blank(limit_rows))

        return lax.cond(jnp.any(permit), active, passive, held_state)

    return lax.scan(advance, state, stacked)


def normaliser_update(queries):

    def update(held_state, pieces, permit):
        top_score, exp_total = held_state
        logits = scores(queries, pieces[0], permit)
        new_top = jnp.maximum(top_score, jnp.max(logits, axis=-1))
        kept_exp = jnp.where(permit[None], jnp.exp(logits - new_top[..., None]), 0.0)
        exp_total = exp_total * jnp.exp(top_score - new_top) + jnp.sum(kept_exp, axis=-1)
        return ((new_top, exp_total), None)

    return update


def output_update(queries, log_total):

    def update(held_state, pieces, permit):
        logits = scores(queries, pieces[0], permit)
        weights_low = jnp.where(permit[None], jnp.exp(logits - log_total[..., None]), 0.0).astype(
            jnp.bfloat16
        )
        return (
            held_state
            + jnp.einsum(
                "hqk,khd->qhd", weights_low, pieces[1], preferred_element_type=jnp.float32
            ),
            None,
        )

    return update


def inner_update(queries, log_total, grad_out_low):

    def update(held_state, pieces, permit):
        logits = scores(queries, pieces[0], permit)
        probs_full = jnp.where(permit[None], jnp.exp(logits - log_total[..., None]), 0.0)
        grad_probs = jnp.einsum(
            "qhd,khd->hqk", grad_out_low, pieces[1], preferred_element_type=jnp.float32
        )
        return (held_state + jnp.sum(probs_full * grad_probs, axis=-1), None)

    return update


def gradient_update(queries, log_total, grad_out_low, inner_sum):

    def update(held_state, pieces, permit):
        logits = scores(queries, pieces[0], permit)
        probs_full = jnp.where(permit[None], jnp.exp(logits - log_total[..., None]), 0.0)
        grad_probs = jnp.einsum(
            "qhd,khd->hqk", grad_out_low, pieces[1], preferred_element_type=jnp.float32
        )
        grad_logits = (probs_full * (grad_probs - inner_sum[..., None]) * ALPHA).astype(
            jnp.bfloat16
        )
        new_state = held_state + jnp.einsum(
            "hqk,khd->qhd", grad_logits, pieces[0], preferred_element_type=jnp.float32
        )
        key_term = jnp.einsum(
            "hqk,qhd->khd", grad_logits, queries, preferred_element_type=jnp.float32
        )
        value_term = jnp.einsum(
            "hqk,qhd->khd",
            probs_full.astype(jnp.bfloat16),
            grad_out_low,
            preferred_element_type=jnp.float32,
        )
        return (new_state, (key_term, value_term))

    return update


def per_device(inputs, w_qkv, w_out, w_up, w_down, norm_gains, norm_biases, block_map, out_grad):
    query_scale = 1.0 / (ALPHA * math.sqrt(DH))
    tokens = inputs.reshape(BLK, D).astype(jnp.float32)
    full_qkv, full_out, full_up, full_down = (
        lax.all_gather(w_qkv, "wsh", axis=0, tiled=True),
        lax.all_gather(w_out, "wsh", axis=0, tiled=True),
        lax.all_gather(w_up, "wsh", axis=0, tiled=True),
        lax.all_gather(w_down, "wsh", axis=0, tiled=True),
    )
    block_entry = block_map.reshape(2)
    local_tags = jnp.stack(
        [
            jnp.full((BLK,), block_entry[0], jnp.int32),
            block_entry[1] + jnp.arange(BLK, dtype=jnp.int32),
        ],
        axis=1,
    )
    first_norm, first_back = jax.vjp(layer_norm, tokens, norm_gains[0], norm_biases[0])
    normed_low = first_norm.astype(jnp.bfloat16)
    projected = jnp.dot(normed_low, full_qkv, preferred_element_type=jnp.float32)
    queries = (projected[:, :D] * query_scale).astype(jnp.bfloat16).reshape(BLK, HEADS, DH)
    key_local = projected[:, D : 2 * D].astype(jnp.bfloat16)
    value_local = projected[:, 2 * D :].astype(jnp.bfloat16)
    start_top = (jnp.full((HEADS, BLK), NEG, jnp.float32), jnp.zeros((HEADS, BLK), jnp.float32))
    start_out = jnp.zeros((BLK, HEADS, DH), jnp.float32)
    key_all, value_all, tag_all = (
        lax.all_gather(key_local, "ctx", axis=0, tiled=True),
        lax.all_gather(value_local, "ctx", axis=0, tiled=True),
        lax.all_gather(local_tags, "ctx", axis=0, tiled=True),
    )
    key_heads = key_all.reshape(-1, HEADS, DH)
    value_heads = value_all.reshape(-1, HEADS, DH)
    top_score, exp_total = sweep_blocks(
        (key_heads, tag_all), local_tags, start_top, normaliser_update(queries), no_output
    )[0]
    log_total = top_score + jnp.log(exp_total)
    attended = sweep_blocks(
        (key_heads, value_heads, tag_all),
        local_tags,
        start_out,
        output_update(queries, log_total),
        no_output,
    )[0]
    attn_low = attended.reshape(BLK, D).astype(jnp.bfloat16)
    branch = jnp.dot(attn_low, full_out, preferred_element_type=jnp.float32)
    post_attn, attn_back = jax.vjp(layer_norm, branch, norm_gains[1], norm_biases[1])
    hidden = tokens + post_attn
    pre_ffn, ffn_back = jax.vjp(layer_norm, hidden, norm_gains[2], norm_biases[2])
    ffn_low = pre_ffn.astype(jnp.bfloat16)
    upward = jnp.dot(ffn_low, full_up, preferred_element_type=jnp.float32)
    activated, gelu_back = jax.vjp(gelu_tanh, upward)
    active_low = activated.astype(jnp.bfloat16)
    downward = jnp.dot(active_low, full_down, preferred_element_type=jnp.float32)
    post_ffn, post_back = jax.vjp(layer_norm, downward, norm_gains[3], norm_biases[3])
    result = (hidden + post_ffn).astype(jnp.bfloat16).reshape(1, 1, BLK, D)
    seed_grad = out_grad.reshape(BLK, D).astype(jnp.float32)
    grad_down_in, gain_grad3, bias_grad3 = post_back(seed_grad)
    down_low = grad_down_in.astype(jnp.bfloat16)
    grad_active = contract_last(down_low, full_down)
    up_low = gelu_back(grad_active)[0].astype(jnp.bfloat16)
    grad_pre_ffn, gain_grad2, bias_grad2 = ffn_back(contract_last(up_low, full_up))
    grad_hidden = seed_grad + grad_pre_ffn
    grad_branch, gain_grad1, bias_grad1 = attn_back(grad_hidden)
    branch_low = grad_branch.astype(jnp.bfloat16)
    grad_out_low = contract_last(branch_low, full_out).astype(jnp.bfloat16).reshape(BLK, HEADS, DH)
    members = (key_heads, value_heads, tag_all)
    inner_sum = sweep_blocks(
        members,
        local_tags,
        jnp.zeros((HEADS, BLK), jnp.float32),
        inner_update(queries, log_total, grad_out_low),
        no_output,
    )[0]
    grad_queries, key_value_terms = sweep_blocks(
        members,
        local_tags,
        start_out,
        gradient_update(queries, log_total, grad_out_low, inner_sum),
        zero_terms,
    )
    key_terms = key_value_terms[0].reshape(-1, D)
    value_terms = key_value_terms[1].reshape(-1, D)
    key_grad, value_grad = (
        lax.psum_scatter(
            key_terms.astype(jnp.bfloat16), "ctx", scatter_dimension=0, tiled=True
        ).astype(jnp.float32),
        lax.psum_scatter(
            value_terms.astype(jnp.bfloat16), "ctx", scatter_dimension=0, tiled=True
        ).astype(jnp.float32),
    )
    qkv_low = jnp.concatenate(
        [
            grad_queries.reshape(BLK, D).astype(jnp.bfloat16) * query_scale,
            key_grad.astype(jnp.bfloat16),
            value_grad.astype(jnp.bfloat16),
        ],
        axis=1,
    )
    grad_tokens, gain_grad0, bias_grad0 = first_back(contract_last(qkv_low, full_qkv))
    grad_input = (grad_hidden + grad_tokens).reshape(1, 1, BLK, D)
    term_qkv = contract_rows(normed_low, qkv_low)
    term_out = contract_rows(attn_low, branch_low)
    term_up = contract_rows(ffn_low, up_low)
    term_down = contract_rows(active_low, down_low)
    shard_qkv, shard_out, shard_up, shard_down = (
        lax.psum_scatter(
            term_qkv.astype(jnp.bfloat16), "wsh", scatter_dimension=0, tiled=True
        ).astype(jnp.float32),
        lax.psum_scatter(
            term_out.astype(jnp.bfloat16), "wsh", scatter_dimension=0, tiled=True
        ).astype(jnp.float32),
        lax.psum_scatter(
            term_up.astype(jnp.bfloat16), "wsh", scatter_dimension=0, tiled=True
        ).astype(jnp.float32),
        lax.psum_scatter(
            term_down.astype(jnp.bfloat16), "wsh", scatter_dimension=0, tiled=True
        ).astype(jnp.float32),
    )
    summed_qkv, summed_out, summed_up, summed_down = (
        lax.psum(shard_qkv.astype(jnp.bfloat16), ("grp", "ctx")).astype(jnp.float32),
        lax.psum(shard_out.astype(jnp.bfloat16), ("grp", "ctx")).astype(jnp.float32),
        lax.psum(shard_up.astype(jnp.bfloat16), ("grp", "ctx")).astype(jnp.float32),
        lax.psum(shard_down.astype(jnp.bfloat16), ("grp", "ctx")).astype(jnp.float32),
    )
    gain_stack = jnp.stack([gain_grad0, gain_grad1, gain_grad2, gain_grad3])
    bias_stack = jnp.stack([bias_grad0, bias_grad1, bias_grad2, bias_grad3])
    gain_total, bias_total = lax.psum((gain_stack, bias_stack), ("grp", "ctx", "wsh"))
    return (
        result,
        grad_input,
        summed_qkv,
        summed_out,
        summed_up,
        summed_down,
        gain_total,
        bias_total,
    )


def solution(mesh):
    return jax.shard_map(
        per_device,
        mesh=mesh,
        in_specs=(
            P("grp", "wsh", "ctx", None),
            P("wsh", None),
            P("wsh", None),
            P("wsh", None),
            P("wsh", None),
            P(),
            P(),
            P("grp", "wsh", "ctx", None),
            P("grp", "wsh", "ctx", None),
        ),
        out_specs=(
            P("grp", "wsh", "ctx", None),
            P("grp", "wsh", "ctx", None),
            P("wsh", None),
            P("wsh", None),
            P("wsh", None),
            P("wsh", None),
            P(),
            P(),
        ),
        check_vma=False,
    )
```

profile of v0, /device:TPU:0, one launch (start us, length us, event | category | flops | bytes accessed | tf_op | source)
XLA Modules:
  0.0 1249.4 jit_solution(280551970439620946)
XLA Ops:
  10.9 47.8 %all-gather.7.cloned.1.call-done = bf16[1024,3072]{1,0:T(8,128)(2,1)} async-done(((bf16[256,3072]{1,0:T(8,128)(2,1)}), bf16[1024,3072]{1,0:T(8,128)(2,1)}) %all-gather.7.cloned.1.call-update) | async-done | bytes 6291472 | tf_op jit(solution)/shard_map/all_gather | solution.py:155
  73.1 14.1 %all_gather.21 = s32[2048,2]{0,1:T(2,128)S(1)} all-gather(s32[512,2]{0,1:T(2,128)S(1)} %stack.6), channel_id=1, replica_groups=mesh['grp'=2,'ctx'=4,'wsh'=4] {'ctx'}, dimensions={0}, use_global_device_ids=true | all-gather | bytes 20480 | tf_op jit(solution)/shard_map/all_gather | solution.py:179
  92.5 57.1 %all-gather.9.cloned.1.call-done = bf16[2048,1024]{1,0:T(8,128)(2,1)} async-done(((bf16[512,1024]{1,0:T(8,128)(2,1)}), bf16[2048,1024]{1,0:T(8,128)(2,1)}) %all-gather.9.cloned.1.call-update) | async-done | bytes 4194320 | tf_op jit(solution)/shard_map/all_gather | solution.py:177
  169.2 10.0 copy.42
  179.2 52.0 %all-gather.11.cloned.1.call-done = bf16[2048,1024]{1,0:T(8,128)(2,1)} async-done(((bf16[512,1024]{1,0:T(8,128)(2,1)}), bf16[2048,1024]{1,0:T(8,128)(2,1)}) %all-gather.11.cloned.1.call-update) | async-done | bytes 4194320 | tf_op jit(solution)/shard_map/all_gather | solution.py:178
  231.1 11.7 reshape.274
  242.9 9.8 copy.44
  252.7 19.8 %while.59 = (s32[]{:T(128)}, f32[16,512]{1,0:T(8,128)S(1)}, f32[16,512]{1,0:T(8,128)S(1)}, s32[4,512,2]{1,2,0:T(2,128)S(1)}, s32[]{:T(128)}, /*index=5*/bf16[4,5...) while((s32[]{:T(128)}, f32[16,512]{1,0:T(8,128)S(1)}, ...), condition=%wide.region_8.9_spmd.clone, body=%wide.region_2.8_spmd.clone.sunk | while | flops 571230208 | bytes 36886224 | solution.py:76
  274.1 24.3 %while.60 = (s32[]{:T(128)}, f32[512,16,64]{0,2,1:T(8,128)}, s32[4,512,2]{1,2,0:T(2,128)S(1)}, s32[]{:T(128)}, bf16[4,512,16,64]{3,2,1,0:T(8,128)(2,1)}, /*index...) while((s32[]{:T(128)}, f32[512,16,64]{0,2,1:T(8,128)}, ...), condition=%wide.region_13.14_spmd.clone, body=%wide.region_9.13_spmd.clone.sunk | while | flops 1096026112 | bytes 11065027 | solution.py:76
  277.2 12.3 conditional.13
  279.2 10.3 bitcast_add_fusion
  313.4 13.1 %fusion.115 = f32[512,4096]{1,0:T(8,128)} fusion(bf16[1024,4096]{1,0:T(8,128)(2,1)} %all-gather.15.cloned.1.call-done, f32[512,1024]{1,0:T(8,128)} %copy-done.1, f32[1024]{0:T(1024)S(1)} %bitcast.299, f32[1024]{0:T(1024)S(1)} %bitcast.289, f32[512]{0:T(512)S(1)} %fusion.106, f32[512]{0:T(512)S(1)} %broadcast_multiply_fusion.1), kind=kOutput, calls=%fused_computation.179 | convolution fusion | flops 4297588736 | bytes 18886656 | tf_op jit(solution)/shard_map/dot_general | solution.py:200
  326.5 46.6 %all-gather.17.cloned.1.call-done = bf16[4096,1024]{1,0:T(8,128)(2,1)} async-done(((bf16[1024,1024]{1,0:T(8,128)(2,1)}), bf16[4096,1024]{1,0:T(8,128)(2,1)}) %all-gather.17.cloned.1.call-update) | async-done | bytes 8388624 | tf_op jit(solution)/shard_map/all_gather | solution.py:158
  373.2 10.5 fusion.130
  388.3 15.7 %fusion.80 = bf16[512,4096]{1,0:T(8,128)(2,1)} fusion(f32[512,4096]{1,0:T(8,128)} %fusion.115, bf16[4096,1024]{1,0:T(8,128)(2,1)} %all-gather.17.cloned.1.call-done, f32[512,1024]{1,0:T(8,128)S(1)} %get-tuple-element.761, f32[512]{0:T(512)S(1)} %negate_multiply_fusion.3), kind=kOutput, calls=%fused_computation.97 | convolution fusion | flops 4337958912 | bytes 23070720 | tf_op jit(solution)/shard_map/dot_general | solution.py:27
  419.4 22.5 %while.61 = (s32[]{:T(128)}, f32[16,512]{1,0:T(8,128)S(1)}, s32[4,512,2]{1,2,0:T(2,128)S(1)}, s32[]{:T(128)}, bf16[4,512,16,64]{1,3,2,0:T(8,128)(2,1)}, /*index=...) while((s32[]{:T(128)}, f32[16,512]{1,0:T(8,128)S(1)}, ...), condition=%wide.region_31.32_spmd.clone, body=%wide.region_26.31_spmd.clone.sunk | while | flops 1099696128 | bytes 38459600 | solution.py:76
  422.4 10.7 conditional.14
  443.2 68.5 %while.62 = (s32[]{:T(128)}, f32[512,16,64]{0,2,1:T(8,128)S(1)}, bf16[4,512,16,64]{1,3,2,0:T(8,128)(2,1)}, bf16[4,512,16,64]{1,3,2,0:T(8,128)(2,1)}, s32[4,512,2...) while((s32[]{:T(128)}, f32[512,16,64]{0,2,1:T(8,128)S(1)}, ...), condition=%wide.region_36.37_spmd.clone, body=%wide.region_32.0_spmd.clone.sunk | while | flops 2740193280 | bytes 94231808 | solution.py:76
  446.3 37.5 %conditional.15 = (f32[512,16,64]{0,2,1:T(8,128)S(1)}, bf16[1,512,16,64]{1,3,2,0:T(8,128)(2,1)}, bf16[1,512,16,64]{1,3,2,0:T(8,128)(2,1)}) conditional(s32[]{:T(128)} %convert_element_type.266, f32[512,16,64]{0,2,1:T(8,128)S(1)} %get-tuple-element.1188, (pred[512,512]{0,1:T(8,128)(4,1)S(1)}, bf16[4,512,16,64]{1,3,2,0:T(8,128)(2,1)}, s32[]{:T(128)}, ...), branch_computations={%region_34.34_spmd, %region_35.35_spmd} | conditional | flops 2739404800 | bytes 89753112 | solution.py:74
  446.3 9.3 fusion.59
  455.7 11.3 fusion.54
  467.0 10.5 fusion.46
  536.1 11.3 convolution_convert_fusion
  548.1 10.8 convolution_convert_fusion.1
  560.1 128.8 %reduce-scatter.9.cloned.1.call-done = bf16[512,1024]{0,1:T(8,128)(2,1)} async-done(((bf16[2048,1024]{0,1:T(8,128)(2,1)}), bf16[512,1024]{0,1:T(8,128)(2,1)}) %reduce-scatter.9.cloned.1.call-update) | async-done | bytes 1048592 | tf_op jit(solution)/shard_map/reduce_scatter | solution.py:237
  688.9 80.3 %reduce-scatter.7.cloned.1.call-done = bf16[512,1024]{0,1:T(8,128)(2,1)} async-done(((bf16[2048,1024]{0,1:T(8,128)(2,1)}), bf16[512,1024]{0,1:T(8,128)(2,1)}) %reduce-scatter.7.cloned.1.call-update) | async-done | bytes 1048592 | tf_op jit(solution)/shard_map/reduce_scatter | solution.py:234
  777.8 25.9 %reduce-scatter.13.cloned.1.call-done = bf16[256,1024]{1,0:T(8,128)(2,1)} async-done(((bf16[1024,1024]{1,0:T(8,128)(2,1)}), bf16[256,1024]{1,0:T(8,128)(2,1)}) %reduce-scatter.13.cloned.1.call-update) | async-done | bytes 524304 | tf_op jit(solution)/shard_map/reduce_scatter | solution.py:259
  803.7 74.4 %reduce-scatter.17.cloned.1.call-done = bf16[1024,1024]{1,0:T(8,128)(2,1)} async-done(((bf16[4096,1024]{1,0:T(8,128)(2,1)}), bf16[1024,1024]{1,0:T(8,128)(2,1)}) %reduce-scatter.17.cloned.1.call-update) | async-done | bytes 2097168 | tf_op jit(solution)/shard_map/reduce_scatter | solution.py:265
  878.1 74.4 %reduce-scatter.15.cloned.1.call-done = bf16[256,4096]{1,0:T(8,128)(2,1)} async-done(((bf16[1024,4096]{1,0:T(8,128)(2,1)}), bf16[256,4096]{1,0:T(8,128)(2,1)}) %reduce-scatter.15.cloned.1.call-update) | async-done | bytes 2097168 | tf_op jit(solution)/shard_map/reduce_scatter | solution.py:262
  952.4 60.9 %reduce-scatter.11.cloned.1.call-done = bf16[256,3072]{1,0:T(8,128)(2,1)} async-done(((bf16[1024,3072]{1,0:T(8,128)(2,1)}), bf16[256,3072]{1,0:T(8,128)(2,1)}) %reduce-scatter.11.cloned.1.call-update) | async-done | bytes 1572880 | tf_op jit(solution)/shard_map/reduce_scatter | solution.py:256
  1024.6 43.2 %all-reduce.1 = (f32[4,1024]{1,0:T(4,128)}, f32[4,1024]{1,0:T(4,128)}) all-reduce(f32[4,1024]{1,0:T(4,128)S(1)} %get-tuple-element.797, f32[4,1024]{1,0:T(4,128)S(1)} %get-tuple-element.798), channel_id=1, replica_groups=mesh['grp'=2,'ctx'=4,'wsh'=4] {'grp','ctx','wsh'}, use_global_device_ids=true, to_apply=%region_53.54 | all-reduce | flops 8192 | bytes 65536 | tf_op jit(solution)/shard_map/psum | solution.py:277
  1071.4 161.8 %all-reduce.5.cloned.1.call-done = (bf16[256,3072]{1,0:T(8,128)(2,1)}, bf16[256,1024]{1,0:T(8,128)(2,1)}, bf16[256,4096]{1,0:T(8,128)(2,1)}, bf16[1024,1024]{1,0:T(8,128)(2,1)}) async-done(((bf16[256,3072]{1,0:T(8,128)(2,1)}, bf16[256,1024]{1,0:T(8,128)(2,1)}, bf16[256,4096]{1,0:T(8,128)(2,1)}, bf16[1024,1024]{1,0:T(8,128)(2,1)}), (bf16[256,3072]{1,0:T(8,128)(2,1)}, bf16[256,1024]{1,0:T(8,128)(2,1)}, ...) | async-done | bytes 6291472 | tf_op jit(solution)/shard_map/psum | solution.py:270
  (318 shorter events, 236.0 us)
Async XLA Ops:
  7.2 51.5 %all-gather.7.cloned.1.call-start = ((), (), s32[]{:S(2)}) async-start(), calls=%async_computation.6 | async-start | bytes 7864320 | tf_op jit(solution)/shard_map/all_gather | solution.py:155
  7.9 141.7 %all-gather.9.cloned.1.call-start = ((), (), s32[]{:S(2)}) async-start(), calls=%async_computation.7 | async-start | bytes 5242880 | tf_op jit(solution)/shard_map/all_gather | solution.py:177
  8.6 58.4 %copy-start.22 = (f32[512]{0:T(512)}, f32[512]{0:T(512)S(1)}, u32[]{:S(2)}) copy-start(f32[512]{0:T(512)S(1)} %broadcast_multiply_fusion.3) | copy-start | bytes 6148
  9.6 57.4 %copy-start.28 = (f32[512]{0:T(512)}, f32[512]{0:T(512)S(1)}, u32[]{:S(2)}) copy-start(f32[512]{0:T(512)S(1)} %fusion.104) | copy-start | bytes 6148
  10.3 56.8 %copy-start.19 = (f32[1,1024]{1,0:T(1,128)}, f32[1,1024]{1,0:T(1,128)S(1)}, u32[]{:S(2)}) copy-start(f32[1,1024]{1,0:T(1,128)S(1)} %get-tuple-element.781) | copy-start | bytes 12292
  10.9 56.2 %copy-start.42 = (f32[1,1024]{1,0:T(1,128)}, f32[1,1024]{1,0:T(1,128)S(1)}, u32[]{:S(2)}) copy-start(f32[1,1024]{1,0:T(1,128)S(1)} %get-tuple-element.785) | copy-start | bytes 12292
  68.6 162.6 %all-gather.11.cloned.1.call-start = ((), (), s32[]{:S(2)}) async-start(), calls=%async_computation.8 | async-start | bytes 5242880 | tf_op jit(solution)/shard_map/all_gather | solution.py:178
  69.3 231.8 %all-gather.13.cloned.1.call-start = ((), (), s32[]{:S(2)}) async-start(), calls=%async_computation.9 | async-start | bytes 2621440 | tf_op jit(solution)/shard_map/all_gather | solution.py:156
  69.9 243.5 %all-gather.15.cloned.1.call-start = ((), (), s32[]{:S(2)}) async-start(), calls=%async_computation.10 | async-start | bytes 10485760 | tf_op jit(solution)/shard_map/all_gather | solution.py:157
  70.5 302.7 %all-gather.17.cloned.1.call-start = ((), (), s32[]{:S(2)}) async-start(), calls=%async_computation.11 | async-start | bytes 10485760 | tf_op jit(solution)/shard_map/all_gather | solution.py:158
  71.1 617.8 %reduce-scatter.9.cloned.1.call-start = ((), (), s32[]{:S(2)}) async-start(), calls=%async_computation.13 | async-start | bytes 5242880 | tf_op jit(solution)/shard_map/reduce_scatter | solution.py:237
  306.4 7.1 copy-start.36
  306.4 7.1 copy-start.44
  306.4 106.1 %copy-start.26 = (f32[512]{0:T(512)}, f32[512]{0:T(512)S(1)}, u32[]{:S(2)}) copy-start(f32[512]{0:T(512)S(1)} %broadcast_multiply_fusion.1) | copy-start | bytes 6148
  308.0 104.5 %copy-start.38 = (f32[512]{0:T(512)}, f32[512]{0:T(512)S(1)}, u32[]{:S(2)}) copy-start(f32[512]{0:T(512)S(1)} %fusion.106) | copy-start | bytes 6148
  386.3 17.7 %slice-start = ((s8[8388608]{0:T(1024)(128)(4,1)}), s8[4194304]{0:T(1024)(128)(4,1)S(1)}, s32[]{:S(2)}) async-start(s8[8388608]{0:T(1024)(128)(4,1)} %bitcast.301), calls=%async_computation.19 | async-start | bytes 8388608
  388.3 15.7 %copy-start.16 = (f32[512,1024]{1,0:T(8,128)}, f32[512,1024]{1,0:T(8,128)S(1)}, u32[]{:S(2)}) copy-start(f32[512,1024]{1,0:T(8,128)S(1)} %get-tuple-element.761) | copy-start | bytes 6291460
  388.3 15.7 %copy-start.46 = (f32[512]{0:T(512)}, f32[512]{0:T(512)S(1)}, u32[]{:S(2)}) copy-start(f32[512]{0:T(512)S(1)} %negate_multiply_fusion.3) | copy-start | bytes 6148
  388.3 15.7 %slice-start.1 = ((s8[8388608]{0:T(1024)(128)(4,1)}), s8[4194304]{0:T(1024)(128)(4,1)S(1)}, s32[]{:S(2)}) async-start(s8[8388608]{0:T(1024)(128)(4,1)} %bitcast.301), calls=%async_computation.20 | async-start | bytes 8388608
  520.8 248.4 %reduce-scatter.7.cloned.1.call-start = ((), (), s32[]{:S(2)}) async-start(), calls=%async_computation.12 | async-start | bytes 5242880 | tf_op jit(solution)/shard_map/reduce_scatter | solution.py:234
  530.0 273.7 %reduce-scatter.13.cloned.1.call-start = ((), (), s32[]{:S(2)}) async-start(), calls=%async_computation.15 | async-start | bytes 2621440 | tf_op jit(solution)/shard_map/reduce_scatter | solution.py:259
  535.5 342.6 %reduce-scatter.17.cloned.1.call-start = ((), (), s32[]{:S(2)}) async-start(), calls=%async_computation.17 | async-start | bytes 10485760 | tf_op jit(solution)/shard_map/reduce_scatter | solution.py:265
  547.5 405.0 %reduce-scatter.15.cloned.1.call-start = ((), (), s32[]{:S(2)}) async-start(), calls=%async_computation.16 | async-start | bytes 10485760 | tf_op jit(solution)/shard_map/reduce_scatter | solution.py:262
  558.9 210.3 %copy-start.5 = (bf16[1,1,512,1024]{3,2,1,0:T(8,128)(2,1)S(1)}, bf16[1,1,512,1024]{3,2,1,0:T(8,128)(2,1)}, u32[]{:S(2)}) copy-start(bf16[1,1,512,1024]{3,2,1,0:T(8,128)(2,1)} %param.25) | copy-start | bytes 3145732
  559.0 210.3 %copy-start.20 = (f32[1,1024]{1,0:T(1,128)S(1)}, f32[1,1024]{1,0:T(1,128)}, u32[]{:S(2)}) copy-start(f32[1,1024]{1,0:T(1,128)} %copy-done.19) | copy-start | bytes 12292
  559.0 210.2 %copy-start.23 = (f32[512]{0:T(512)S(1)}, f32[512]{0:T(512)}, u32[]{:S(2)}) copy-start(f32[512]{0:T(512)} %copy-done.22) | copy-start | bytes 6148
  559.0 210.2 %copy-start.29 = (f32[512]{0:T(512)S(1)}, f32[512]{0:T(512)}, u32[]{:S(2)}) copy-start(f32[512]{0:T(512)} %copy-done.28) | copy-start | bytes 6148
  559.0 210.2 %copy-start.43 = (f32[1,1024]{1,0:T(1,128)S(1)}, f32[1,1024]{1,0:T(1,128)}, u32[]{:S(2)}) copy-start(f32[1,1024]{1,0:T(1,128)} %copy-done.42) | copy-start | bytes 12292
  559.0 454.4 %reduce-scatter.11.cloned.1.call-start = ((), (), s32[]{:S(2)}) async-start(), calls=%async_computation.14 | async-start | bytes 7864320 | tf_op jit(solution)/shard_map/reduce_scatter | solution.py:256
  777.6 455.6 %all-reduce.5.cloned.1.call-start = ((), (), s32[]{:S(2)}) async-start(), calls=%async_computation.18 | async-start | bytes 12582912 | tf_op jit(solution)/shard_map/psum | solution.py:270
  1014.9 7.3 copy-start.25
  1022.2 45.6 %copy-start.7 = (f32[512,1024]{1,0:T(8,128)S(1)}, f32[512,1024]{1,0:T(8,128)}, u32[]{:S(2)}) copy-start(f32[512,1024]{1,0:T(8,128)} %copy-done.6) | copy-start | bytes 6291460
  (34 other events, 55.5 us)
Sparse Core Ops, SparseCore 0:
  9.6 49.0 all-gather.6
  68.7 80.8 all-gather.8
  151.8 79.3 all-gather.10
  232.5 21.1 all-gather.12
  255.1 58.2 all-gather.14
  314.8 58.2 all-gather.16
  520.9 167.9 reduce-scatter.8
  691.9 77.2 reduce-scatter.6
  771.7 31.9 reduce-scatter.12
  806.3 71.7 reduce-scatter.16
  880.7 71.7 reduce-scatter.14
  955.0 58.3 reduce-scatter.10
  1017.8 215.3 all-reduce.4
where the time goes:
time: 1250 us
  waiting for transfers between devices  818 us (65%)
  matrix products  165 us (13%)
  local copies, waits for them, and re-layouts  112 us (9%)
  other arithmetic  69.5 us (6%)
  blocking collectives  57.3 us (5%)
  between operations  14.7 us (1%)
    psum x1, waiting for transfers between devices, per_device(): lax.psum(shard_qkv.astype(jnp.bfloat16), ('grp', 'ctx')).astype(jnp.float32)  162 us
    reduce_scatter x1, waiting for transfers between devices, per_device(): lax.psum_scatter(value_terms.astype(jnp.bfloat16), 'ctx', scatter_dimensi...  129 us
    reduce_scatter x1, waiting for transfers between devices, per_device(): lax.psum_scatter(key_terms.astype(jnp.bfloat16), 'ctx', scatter_dimension...  80.3 us
    reduce_scatter x1, waiting for transfers between devices, per_device(): lax.psum_scatter(term_down.astype(jnp.bfloat16), 'wsh', scatter_dimension...  74.4 us
    reduce_scatter x1, waiting for transfers between devices, per_device(): lax.psum_scatter(term_up.astype(jnp.bfloat16), 'wsh', scatter_dimension=0...  74.4 us
    reduce_scatter x1, waiting for transfers between devices, per_device(): lax.psum_scatter(term_qkv.astype(jnp.bfloat16), 'wsh', scatter_dimension=...  60.9 us
    all_gather x1, waiting for transfers between devices, per_device(): lax.all_gather(key_local, 'ctx', axis=0, tiled=True)  57.1 us
    all_gather x1, waiting for transfers between devices, per_device(): lax.all_gather(value_local, 'ctx', axis=0, tiled=True)  52 us
  transfers between devices with their start and end apart: 13, of which 12 were waited for; matrix products, arithmetic and copies ran while one was open for 14% of the time, Pallas kernels for 0%

commit v1 on v0

--- a/solution.py
+++ b/solution.py
@@ -267,7 +267,9 @@
         ).astype(jnp.float32),
     )
     summed_qkv, summed_out, summed_up, summed_down = (
-        lax.psum(shard_qkv.astype(jnp.bfloat16), ("grp", "ctx")).astype(jnp.float32),
+        jnp.sum(lax.all_gather(shard_qkv.astype(jnp.bfloat16), axis_name=("grp", "ctx")), 0).astype(
+            jnp.float32
+        ),
         lax.psum(shard_out.astype(jnp.bfloat16), ("grp", "ctx")).astype(jnp.float32),
         lax.psum(shard_up.astype(jnp.bfloat16), ("grp", "ctx")).astype(jnp.float32),
         lax.psum(shard_down.astype(jnp.bfloat16), ("grp", "ctx")).astype(jnp.float32),

time: 1250 us -> 1390 us (1.11)
  waiting for transfers between devices: 818 us -> 942 us
    all_gather x0 -> x1, waiting for transfers between devices: none -> 168 us  [per_device(): lax.all_gather(shard_qkv.astype(jnp.bfloat16), axis_name=('grp', 'ctx'))]
    psum x1, waiting for transfers between devices: 162 us -> 117 us  [per_device(): lax.psum(shard_out.astype(jnp.bfloat16), ('grp', 'ctx')).astype(jnp.float32)]
    unnamed x112 -> x108, local copies, waits for them, and re-layouts: 46.7 us -> 45.2 us
  transfers between devices with their start and end apart: 13 -> 14, of which waited for: 12 -> 13; matrix products, arithmetic and copies ran while one was open for 14% -> 13% of each run, Pallas kernels for 0% -> 0%
where the time goes in v1:
time: 1390 us; the launch traced here: 1380 us
  waiting for transfers between devices  942 us (68%)
  matrix products  165 us (12%)
  local copies, waits for them, and re-layouts  111 us (8%)
  other arithmetic  77.9 us (6%)
  blocking collectives  59.4 us (4%)
  between operations  14.8 us (1%)
    all_gather x1, waiting for transfers between devices, per_device(): lax.all_gather(shard_qkv.astype(jnp.bfloat16), axis_name=('grp', 'ctx'))  168 us
    reduce_scatter x1, waiting for transfers between devices, per_device(): lax.psum_scatter(value_terms.astype(jnp.bfloat16), 'ctx', scatter_dimensi...  129 us
    psum x1, waiting for transfers between devices, per_device(): lax.psum(shard_out.astype(jnp.bfloat16), ('grp', 'ctx')).astype(jnp.float32)  117 us
    reduce_scatter x1, waiting for transfers between devices, per_device(): lax.psum_scatter(key_terms.astype(jnp.bfloat16), 'ctx', scatter_dimension...  80.3 us
    reduce_scatter x1, waiting for transfers between devices, per_device(): lax.psum_scatter(term_up.astype(jnp.bfloat16), 'wsh', scatter_dimension=0...  74.4 us
    reduce_scatter x1, waiting for transfers between devices, per_device(): lax.psum_scatter(term_down.astype(jnp.bfloat16), 'wsh', scatter_dimension...  74.3 us
    reduce_scatter x1, waiting for transfers between devices, per_device(): lax.psum_scatter(term_qkv.astype(jnp.bfloat16), 'wsh', scatter_dimension=...  60.7 us
    all_gather x1, waiting for transfers between devices, per_device(): lax.all_gather(key_local, 'ctx', axis=0, tiled=True)  57.1 us
  transfers between devices with their start and end apart: 14, of which 13 were waited for; matrix products, arithmetic and copies ran while one was open for 13% of the time, Pallas kernels for 0%

profile of v1, /device:TPU:0, one launch (start us, length us, event | category | flops | bytes accessed | tf_op | source)
XLA Modules:
  0.0 1381.4 jit_solution(14990254059145719077)
XLA Ops:
  10.9 47.8 %all-gather.9.cloned.1.call-done = bf16[1024,3072]{1,0:T(8,128)(2,1)} async-done(((bf16[256,3072]{1,0:T(8,128)(2,1)}), bf16[1024,3072]{1,0:T(8,128)(2,1)}) %all-gather.9.cloned.1.call-update) | async-done | bytes 6291472 | tf_op jit(solution)/shard_map/all_gather | solution.py:155
  73.1 14.2 %all_gather.27 = s32[2048,2]{0,1:T(2,128)S(1)} all-gather(s32[512,2]{0,1:T(2,128)S(1)} %stack.6), channel_id=1, replica_groups=mesh['grp'=2,'ctx'=4,'wsh'=4] {'ctx'}, dimensions={0}, use_global_device_ids=true | all-gather | bytes 20480 | tf_op jit(solution)/shard_map/all_gather | solution.py:179
  92.5 57.1 %all-gather.11.cloned.1.call-done = bf16[2048,1024]{1,0:T(8,128)(2,1)} async-done(((bf16[512,1024]{1,0:T(8,128)(2,1)}), bf16[2048,1024]{1,0:T(8,128)(2,1)}) %all-gather.11.cloned.1.call-update) | async-done | bytes 4194320 | tf_op jit(solution)/shard_map/all_gather | solution.py:177
  169.2 10.0 copy.42
  179.2 52.0 %all-gather.13.cloned.1.call-done = bf16[2048,1024]{1,0:T(8,128)(2,1)} async-done(((bf16[512,1024]{1,0:T(8,128)(2,1)}), bf16[2048,1024]{1,0:T(8,128)(2,1)}) %all-gather.13.cloned.1.call-update) | async-done | bytes 4194320 | tf_op jit(solution)/shard_map/all_gather | solution.py:178
  231.1 11.7 reshape.275
  242.9 9.8 copy.44
  252.7 19.8 %while.59 = (s32[]{:T(128)}, f32[16,512]{1,0:T(8,128)S(1)}, f32[16,512]{1,0:T(8,128)S(1)}, s32[4,512,2]{1,2,0:T(2,128)S(1)}, s32[]{:T(128)}, /*index=5*/bf16[4,5...) while((s32[]{:T(128)}, f32[16,512]{1,0:T(8,128)S(1)}, ...), condition=%wide.region_8.9_spmd.clone, body=%wide.region_2.8_spmd.clone.sunk | while | flops 571230208 | bytes 36886224 | solution.py:76
  274.1 24.2 %while.60 = (s32[]{:T(128)}, f32[512,16,64]{0,2,1:T(8,128)}, s32[4,512,2]{1,2,0:T(2,128)S(1)}, s32[]{:T(128)}, bf16[4,512,16,64]{3,2,1,0:T(8,128)(2,1)}, /*index...) while((s32[]{:T(128)}, f32[512,16,64]{0,2,1:T(8,128)}, ...), condition=%wide.region_13.14_spmd.clone, body=%wide.region_9.13_spmd.clone.sunk | while | flops 1096026112 | bytes 11065027 | solution.py:76
  277.2 12.3 conditional.13
  279.1 10.3 bitcast_add_fusion
  313.4 13.1 fusion.115
  326.6 46.6 %all-gather.19.cloned.1.call-done = bf16[4096,1024]{1,0:T(8,128)(2,1)} async-done(((bf16[1024,1024]{1,0:T(8,128)(2,1)}), bf16[4096,1024]{1,0:T(8,128)(2,1)}) %all-gather.19.cloned.1.call-update) | async-done | bytes 8388624 | tf_op jit(solution)/shard_map/all_gather | solution.py:158
  373.2 10.5 fusion.130
  388.3 15.6 %fusion.80 = bf16[512,4096]{1,0:T(8,128)(2,1)} fusion(f32[512,4096]{1,0:T(8,128)} %fusion.115, bf16[4096,1024]{1,0:T(8,128)(2,1)} %all-gather.19.cloned.1.call-done, f32[512,1024]{1,0:T(8,128)S(1)} %get-tuple-element.760, f32[512]{0:T(512)S(1)} %negate_multiply_fusion.3), kind=kOutput, calls=%fused_computation.97 | convolution fusion | flops 4337958912 | bytes 23070720 | tf_op jit(solution)/shard_map/dot_general | solution.py:27
  419.4 22.1 %while.61 = (s32[]{:T(128)}, f32[16,512]{1,0:T(8,128)S(1)}, s32[4,512,2]{1,2,0:T(2,128)S(1)}, s32[]{:T(128)}, bf16[4,512,16,64]{1,3,2,0:T(8,128)(2,1)}, /*index=...) while((s32[]{:T(128)}, f32[16,512]{1,0:T(8,128)S(1)}, ...), condition=%wide.region_31.32_spmd.clone, body=%wide.region_26.31_spmd.clone.sunk | while | flops 1099696128 | bytes 38459600 | solution.py:76
  422.2 10.7 conditional.14
  442.7 68.3 %while.62 = (s32[]{:T(128)}, f32[512,16,64]{0,2,1:T(8,128)S(1)}, bf16[4,512,16,64]{1,3,2,0:T(8,128)(2,1)}, bf16[4,512,16,64]{1,3,2,0:T(8,128)(2,1)}, s32[4,512,2...) while((s32[]{:T(128)}, f32[512,16,64]{0,2,1:T(8,128)S(1)}, ...), condition=%wide.region_36.37_spmd.clone, body=%wide.region_32.0_spmd.clone.sunk | while | flops 2740193280 | bytes 94231808 | solution.py:76
  445.8 37.6 %conditional.15 = (f32[512,16,64]{0,2,1:T(8,128)S(1)}, bf16[1,512,16,64]{1,3,2,0:T(8,128)(2,1)}, bf16[1,512,16,64]{1,3,2,0:T(8,128)(2,1)}) conditional(s32[]{:T(128)} %convert_element_type.268, f32[512,16,64]{0,2,1:T(8,128)S(1)} %get-tuple-element.1187, (pred[512,512]{0,1:T(8,128)(4,1)S(1)}, bf16[4,512,16,64]{1,3,2,0:T(8,128)(2,1)}, s32[]{:T(128)}, ...), branch_computations={%region_34.34_spmd, %region_35.35_spmd} | conditional | flops 2739404800 | bytes 89753112 | solution.py:74
  455.1 11.3 fusion.54
  466.4 10.5 fusion.46
  535.5 11.3 convolution_convert_fusion
  547.5 10.8 convolution_convert_fusion.1
  559.5 128.8 %reduce-scatter.9.cloned.1.call-done = bf16[512,1024]{0,1:T(8,128)(2,1)} async-done(((bf16[2048,1024]{0,1:T(8,128)(2,1)}), bf16[512,1024]{0,1:T(8,128)(2,1)}) %reduce-scatter.9.cloned.1.call-update) | async-done | bytes 1048592 | tf_op jit(solution)/shard_map/reduce_scatter | solution.py:237
  688.3 80.3 %reduce-scatter.7.cloned.1.call-done = bf16[512,1024]{0,1:T(8,128)(2,1)} async-done(((bf16[2048,1024]{0,1:T(8,128)(2,1)}), bf16[512,1024]{0,1:T(8,128)(2,1)}) %reduce-scatter.7.cloned.1.call-update) | async-done | bytes 1048592 | tf_op jit(solution)/shard_map/reduce_scatter | solution.py:234
  777.0 26.1 %reduce-scatter.13.cloned.1.call-done = bf16[256,1024]{1,0:T(8,128)(2,1)} async-done(((bf16[1024,1024]{1,0:T(8,128)(2,1)}), bf16[256,1024]{1,0:T(8,128)(2,1)}) %reduce-scatter.13.cloned.1.call-update) | async-done | bytes 524304 | tf_op jit(solution)/shard_map/reduce_scatter | solution.py:259
  803.1 74.3 %reduce-scatter.17.cloned.1.call-done = bf16[1024,1024]{1,0:T(8,128)(2,1)} async-done(((bf16[4096,1024]{1,0:T(8,128)(2,1)}), bf16[1024,1024]{1,0:T(8,128)(2,1)}) %reduce-scatter.17.cloned.1.call-update) | async-done | bytes 2097168 | tf_op jit(solution)/shard_map/reduce_scatter | solution.py:265
  877.4 74.4 %reduce-scatter.15.cloned.1.call-done = bf16[256,4096]{1,0:T(8,128)(2,1)} async-done(((bf16[1024,4096]{1,0:T(8,128)(2,1)}), bf16[256,4096]{1,0:T(8,128)(2,1)}) %reduce-scatter.15.cloned.1.call-update) | async-done | bytes 2097168 | tf_op jit(solution)/shard_map/reduce_scatter | solution.py:262
  952.1 60.7 %reduce-scatter.11.cloned.1.call-done = bf16[256,3072]{1,0:T(8,128)(2,1)} async-done(((bf16[1024,3072]{1,0:T(8,128)(2,1)}), bf16[256,3072]{1,0:T(8,128)(2,1)}) %reduce-scatter.11.cloned.1.call-update) | async-done | bytes 1572880 | tf_op jit(solution)/shard_map/reduce_scatter | solution.py:256
  1022.7 45.2 %all-reduce.1 = (f32[4,1024]{1,0:T(4,128)}, f32[4,1024]{1,0:T(4,128)}) all-reduce(f32[4,1024]{1,0:T(4,128)S(1)} %get-tuple-element.796, f32[4,1024]{1,0:T(4,128)S(1)} %get-tuple-element.797), channel_id=1, replica_groups=mesh['grp'=2,'ctx'=4,'wsh'=4] {'grp','ctx','wsh'}, use_global_device_ids=true, to_apply=%region_53.54 | all-reduce | flops 8192 | bytes 65536 | tf_op jit(solution)/shard_map/psum | solution.py:279
  1071.5 116.6 %all-reduce.5.cloned.1.call-done = (bf16[256,1024]{1,0:T(8,128)(2,1)}, bf16[256,4096]{1,0:T(8,128)(2,1)}, bf16[1024,1024]{1,0:T(8,128)(2,1)}) async-done(((bf16[256,1024]{1,0:T(8,128)(2,1)}, bf16[256,4096]{1,0:T(8,128)(2,1)}, bf16[1024,1024]{1,0:T(8,128)(2,1)}), (bf16[256,1024]{1,0:T(8,128)(2,1)}, bf16[256,4096]{1,0:T(8,128)(2,1)}, bf16[1024,1024]{1,0:T(8,128)(2,1)})) %all-reduce.5.cloned.1.call-update) | async-done | bytes 4718608 | tf_op jit(solution)/shard_map/psum | solution.py:273
  1197.0 168.4 %all-gather.21.cloned.1.call-done = bf16[2048,3072]{1,0:T(8,128)(2,1)} async-done(((bf16[256,3072]{1,0:T(8,128)(2,1)}), bf16[2048,3072]{1,0:T(8,128)(2,1)}) %all-gather.21.cloned.1.call-update) | async-done | bytes 12582928 | tf_op jit(solution)/shard_map/all_gather | solution.py:270
  (318 shorter events, 252.6 us)
Async XLA Ops:
  7.2 51.5 %all-gather.9.cloned.1.call-start = ((), (), s32[]{:S(2)}) async-start(), calls=%async_computation.6 | async-start | bytes 7864320 | tf_op jit(solution)/shard_map/all_gather | solution.py:155
  7.9 141.7 %all-gather.11.cloned.1.call-start = ((), (), s32[]{:S(2)}) async-start(), calls=%async_computation.7 | async-start | bytes 5242880 | tf_op jit(solution)/shard_map/all_gather | solution.py:177
  8.6 58.4 %copy-start.20 = (f32[512]{0:T(512)}, f32[512]{0:T(512)S(1)}, u32[]{:S(2)}) copy-start(f32[512]{0:T(512)S(1)} %broadcast_multiply_fusion.3) | copy-start | bytes 6148
  9.6 57.4 %copy-start.26 = (f32[512]{0:T(512)}, f32[512]{0:T(512)S(1)}, u32[]{:S(2)}) copy-start(f32[512]{0:T(512)S(1)} %fusion.104) | copy-start | bytes 6148
  10.3 56.8 %copy-start.17 = (f32[1,1024]{1,0:T(1,128)}, f32[1,1024]{1,0:T(1,128)S(1)}, u32[]{:S(2)}) copy-start(f32[1,1024]{1,0:T(1,128)S(1)} %get-tuple-element.780) | copy-start | bytes 12292
  10.9 56.2 %copy-start.40 = (f32[1,1024]{1,0:T(1,128)}, f32[1,1024]{1,0:T(1,128)S(1)}, u32[]{:S(2)}) copy-start(f32[1,1024]{1,0:T(1,128)S(1)} %get-tuple-element.784) | copy-start | bytes 12292
  68.6 162.5 %all-gather.13.cloned.1.call-start = ((), (), s32[]{:S(2)}) async-start(), calls=%async_computation.8 | async-start | bytes 5242880 | tf_op jit(solution)/shard_map/all_gather | solution.py:178
  69.3 231.7 %all-gather.15.cloned.1.call-start = ((), (), s32[]{:S(2)}) async-start(), calls=%async_computation.9 | async-start | bytes 2621440 | tf_op jit(solution)/shard_map/all_gather | solution.py:156
  69.9 243.5 %all-gather.17.cloned.1.call-start = ((), (), s32[]{:S(2)}) async-start(), calls=%async_computation.10 | async-start | bytes 10485760 | tf_op jit(solution)/shard_map/all_gather | solution.py:157
  70.5 302.7 %all-gather.19.cloned.1.call-start = ((), (), s32[]{:S(2)}) async-start(), calls=%async_computation.11 | async-start | bytes 10485760 | tf_op jit(solution)/shard_map/all_gather | solution.py:158
  71.1 617.2 %reduce-scatter.9.cloned.1.call-start = ((), (), s32[]{:S(2)}) async-start(), calls=%async_computation.13 | async-start | bytes 5242880 | tf_op jit(solution)/shard_map/reduce_scatter | solution.py:237
  306.3 106.1 %copy-start.24 = (f32[512]{0:T(512)}, f32[512]{0:T(512)S(1)}, u32[]{:S(2)}) copy-start(f32[512]{0:T(512)S(1)} %broadcast_multiply_fusion.1) | copy-start | bytes 6148
  307.9 104.5 %copy-start.36 = (f32[512]{0:T(512)}, f32[512]{0:T(512)S(1)}, u32[]{:S(2)}) copy-start(f32[512]{0:T(512)S(1)} %fusion.106) | copy-start | bytes 6148
  386.4 17.6 %slice-start = ((s8[8388608]{0:T(1024)(128)(4,1)}), s8[4194304]{0:T(1024)(128)(4,1)S(1)}, s32[]{:S(2)}) async-start(s8[8388608]{0:T(1024)(128)(4,1)} %bitcast.303), calls=%async_computation.20 | async-start | bytes 8388608
  388.3 15.6 %copy-start.15 = (f32[512,1024]{1,0:T(8,128)}, f32[512,1024]{1,0:T(8,128)S(1)}, u32[]{:S(2)}) copy-start(f32[512,1024]{1,0:T(8,128)S(1)} %get-tuple-element.760) | copy-start | bytes 6291460
  388.3 15.6 %copy-start.44 = (f32[512]{0:T(512)}, f32[512]{0:T(512)S(1)}, u32[]{:S(2)}) copy-start(f32[512]{0:T(512)S(1)} %negate_multiply_fusion.3) | copy-start | bytes 6148
  388.3 15.6 %slice-start.1 = ((s8[8388608]{0:T(1024)(128)(4,1)}), s8[4194304]{0:T(1024)(128)(4,1)S(1)}, s32[]{:S(2)}) async-start(s8[8388608]{0:T(1024)(128)(4,1)} %bitcast.303), calls=%async_computation.21 | async-start | bytes 8388608
  520.2 248.4 %reduce-scatter.7.cloned.1.call-start = ((), (), s32[]{:S(2)}) async-start(), calls=%async_computation.12 | async-start | bytes 5242880 | tf_op jit(solution)/shard_map/reduce_scatter | solution.py:234
  529.4 273.7 %reduce-scatter.13.cloned.1.call-start = ((), (), s32[]{:S(2)}) async-start(), calls=%async_computation.15 | async-start | bytes 2621440 | tf_op jit(solution)/shard_map/reduce_scatter | solution.py:259
  534.8 342.6 %reduce-scatter.17.cloned.1.call-start = ((), (), s32[]{:S(2)}) async-start(), calls=%async_computation.17 | async-start | bytes 10485760 | tf_op jit(solution)/shard_map/reduce_scatter | solution.py:265
  546.9 404.9 %reduce-scatter.15.cloned.1.call-start = ((), (), s32[]{:S(2)}) async-start(), calls=%async_computation.16 | async-start | bytes 10485760 | tf_op jit(solution)/shard_map/reduce_scatter | solution.py:262
  558.3 210.2 %copy-start.5 = (bf16[1,1,512,1024]{3,2,1,0:T(8,128)(2,1)S(1)}, bf16[1,1,512,1024]{3,2,1,0:T(8,128)(2,1)}, u32[]{:S(2)}) copy-start(bf16[1,1,512,1024]{3,2,1,0:T(8,128)(2,1)} %param.25) | copy-start | bytes 3145732
  558.3 210.2 %copy-start.18 = (f32[1,1024]{1,0:T(1,128)S(1)}, f32[1,1024]{1,0:T(1,128)}, u32[]{:S(2)}) copy-start(f32[1,1024]{1,0:T(1,128)} %copy-done.17) | copy-start | bytes 12292
  558.4 210.2 %copy-start.21 = (f32[512]{0:T(512)S(1)}, f32[512]{0:T(512)}, u32[]{:S(2)}) copy-start(f32[512]{0:T(512)} %copy-done.20) | copy-start | bytes 6148
  558.4 210.2 %copy-start.27 = (f32[512]{0:T(512)S(1)}, f32[512]{0:T(512)}, u32[]{:S(2)}) copy-start(f32[512]{0:T(512)} %copy-done.26) | copy-start | bytes 6148
  558.4 210.2 %copy-start.41 = (f32[1,1024]{1,0:T(1,128)S(1)}, f32[1,1024]{1,0:T(1,128)}, u32[]{:S(2)}) copy-start(f32[1,1024]{1,0:T(1,128)} %copy-done.40) | copy-start | bytes 12292
  558.4 454.4 %reduce-scatter.11.cloned.1.call-start = ((), (), s32[]{:S(2)}) async-start(), calls=%async_computation.14 | async-start | bytes 7864320 | tf_op jit(solution)/shard_map/reduce_scatter | solution.py:256
  776.9 411.1 %all-reduce.5.cloned.1.call-start = ((), (), s32[]{:S(2)}) async-start(), calls=%async_computation.19 | async-start | bytes 9437184 | tf_op jit(solution)/shard_map/psum | solution.py:273
  951.8 61.0 %copy-start.9 = (bf16[1,1,512,1024]{3,2,1,0:T(8,128)(2,1)S(1)}, bf16[1,1,512,1024]{3,2,1,0:T(8,128)(2,1)}, u32[]{:S(2)}) copy-start(bf16[1,1,512,1024]{3,2,1,0:T(8,128)(2,1)} %param.33) | copy-start | bytes 3145732
  951.8 61.2 %copy-start.16 = (bf16[512,16,64]{0,2,1:T(8,128)(2,1)S(1)}, bf16[512,16,64]{0,2,1:T(8,128)(2,1)}, u32[]{:S(2)}) copy-start(bf16[512,16,64]{0,2,1:T(8,128)(2,1)} %convert_multiply_fusion) | copy-start | bytes 3145732
  951.8 413.6 %all-gather.21.cloned.1.call-start = ((), (), s32[]{:S(2)}) async-start(), calls=%async_computation.18 | async-start | bytes 14155776 | tf_op jit(solution)/shard_map/all_gather | solution.py:270
  1020.3 47.6 %copy-start.7 = (f32[512,1024]{1,0:T(8,128)S(1)}, f32[512,1024]{1,0:T(8,128)}, u32[]{:S(2)}) copy-start(f32[512,1024]{1,0:T(8,128)} %copy-done.6) | copy-start | bytes 6291460
  (33 other events, 71.8 us)
Sparse Core Ops, SparseCore 0:
  9.6 49.0 all-gather.8
  68.7 80.8 all-gather.10
  151.8 79.3 all-gather.12
  232.6 21.1 all-gather.14
  255.1 58.2 all-gather.16
  314.9 58.2 all-gather.18
  520.3 167.9 reduce-scatter.8
  691.3 77.2 reduce-scatter.6
  771.1 31.9 reduce-scatter.12
  805.7 71.6 reduce-scatter.16
  880.0 71.7 reduce-scatter.14
  954.3 58.3 reduce-scatter.10
  1016.7 171.2 all-reduce.4
  1190.0 175.3 all-gather.20
